TPU v7x, 512 devices: a whole 4x8x8 slice. The times are simulated.
512 devices in a mesh: op: 64 (over x, y, core), sec: 8 (over z).
Axes of the slice: x: 4, y: 8, z: 8, core: 2. Of those that a mesh axis runs over, the one named last changes fastest.
Arguments:
- wavefunction: bfloat16 [8, 512, 512], P('sec', 'op'), may hold values from -6 to 6
- left_ops: bfloat16 [2048, 512, 512], P(('op', 'sec')), may hold values from -0.25 to 0.25
- right_ops: bfloat16 [2048, 512, 512], P(('op', 'sec')), may hold values from -0.25 to 0.25
- in_sector: int32 [2048], P(('op', 'sec')), may hold values from 0 to 7
- counts: int32 [64, 8], replicated, may hold values from 1 to 4
Outputs:
- applied: bfloat16 [8, 512, 512], P('sec', 'op')
Inputs may be any that keep to these rules, and one draw needn't show every extreme that they name: `counts`: a device's live terms are its first slots, as many as its count.
All inputs are finite; a program needn't handle non-finite values.
Results may differ from a plain program's by a relative error of at most 0.0049.
Values may be sent and summed in bfloat16 or wider, within the bound.
A program may use at most 64 MiB of HBM per device.

v0:
```python
import jax
import jax.numpy as jnp
from jax import lax
from jax.sharding import PartitionSpec as P


def joined_along(parts, dim):
    dims = list(parts.shape[1:])
    dims[dim] *= parts.shape[0]
    return jnp.moveaxis(parts, 0, dim).reshape(dims)


def copy_for_each(value, axis):
    devices = lax.axis_size(axis)
    return lax.all_to_all(
        jnp.broadcast_to(value[None], (devices, *value.shape)), axis, 0, 0, tiled=True
    )


def gathered_copies(value, axis, dim):
    return joined_along(copy_for_each(value, axis), dim)


def in_blocks(value, dim, devices):
    before, after = (value.shape[:dim], value.shape[dim + 1 :])
    return jnp.moveaxis(value.reshape(*before, devices, -1, *after), dim, 0)


def sum_at_owner(value, axis, dim):
    devices = lax.axis_size(axis)
    parts = lax.all_to_all(in_blocks(value, dim, devices), axis, 0, 0, tiled=True)
    return jnp.sum(parts, axis=0)


def shards(wavefunction, left_ops, right_ops, in_sector, counts):
    op_devices = lax.axis_size("op")
    op_place = lax.axis_index("op")
    sec_place = lax.axis_index("sec")
    row_pieces = gathered_copies(wavefunction, "sec", 0)
    wanted = gathered_copies(in_sector, "op", 0).reshape(op_devices, -1)
    picked = jnp.take(row_pieces, wanted.T, axis=0)
    arrived = lax.all_to_all(picked, "op", split_axis=1, concat_axis=1, tiled=True)
    blocks = arrived.reshape(arrived.shape[0], -1, arrived.shape[-1])

    def block_of(slot_index):
        return lax.dynamic_index_in_dim(blocks, slot_index, 0, keepdims=False)

    own_count = counts[op_place, sec_place]

    def local_step(slot_index, summed):
        left_block = lax.dynamic_index_in_dim(left_ops, slot_index, 0, keepdims=False)
        right_block = lax.dynamic_index_in_dim(right_ops, slot_index, 0, keepdims=False)
        halfway = jnp.dot(
            left_block, block_of(slot_index), preferred_element_type=jnp.float32
        ).astype(jnp.bfloat16)
        product = lax.dot_general(
            halfway, right_block, (((1,), (1,)), ((), ())), preferred_element_type=jnp.float32
        )
        return summed + product

    initial = jnp.zeros((left_ops.shape[1], right_ops.shape[1]), jnp.float32)
    summed = lax.fori_loop(0, own_count, local_step, initial)
    shares = sum_at_owner(summed, "op", 0)
    factor = (op_devices * left_ops.shape[0]) ** (-0.5)
    return (shares * factor).astype(jnp.bfloat16)[None]


def solution(mesh):
    placed = (
        P("sec", "op", None),
        P(("op", "sec"), None, None),
        P(("op", "sec"), None, None),
        P(("op", "sec")),
        P(),
    )
    return jax.shard_map(
        shards, mesh=mesh, in_specs=placed, out_specs=P("sec", "op", None), check_vma=False
    )
```

profile of v0, /device:TPU:1, one launch (start us, length us, event | category | flops | bytes accessed | tf_op | source)
XLA Modules:
  0.0 148.6 jit_solution(1232492047563994521)
XLA Ops:
  0.0 0.7 broadcast_in_dim.31
  0.7 20.7 %all_to_all.24 = s32[64,1,4]{2,1,0:T(1,128)S(1)} all-to-all(s32[64,1,4]{2,1,0:T(1,128)S(1)} %broadcast_in_dim.31), channel_id=1, replica_groups=mesh['op'=64,'sec'=8] {'op'}, dimensions={0} | all-to-all | bytes 2048 | tf_op jit(solution)/shard_map/all_to_all | solution.py:15
  21.4 1.3 broadcast_in_dim.34
  22.7 10.0 %all-to-all-start.1 = ((bf16[8,1,8,512]{3,2,1,0:T(8,128)(2,1)}), bf16[8,1,8,512]{3,2,1,0:T(8,128)(2,1)S(1)}, u32[]{:S(2)}, u32[]{:S(2)}) async-start(bf16[8,1,8,512]{3,2,1,0:T(8,128)(2,1)} %broadcast_in_dim.34), calls=%async_computation.1 | async-start | bytes 131072 | tf_op jit(solution)/shard_map/all_to_all | solution.py:15
  32.8 0.1 copy.7
  32.9 0.1 reshape.41
  32.9 0.1 copy.6
  33.0 7.0 %all-to-all-done.1 = bf16[8,1,8,512]{3,2,1,0:T(8,128)(2,1)S(1)} async-done(((bf16[8,1,8,512]{3,2,1,0:T(8,128)(2,1)}), bf16[8,1,8,512]{3,2,1,0:T(8,128)(2,1)S(1)}, u32[]{:S(2)}, u32[]{:S(2)}) %all-to-all-start.1) | async-done | bytes 65568 | tf_op jit(solution)/shard_map/all_to_all | solution.py:15
  40.1 0.8 gather_fusion
  40.8 0.5 broadcast_select_fusion
  41.3 1.6 %copy.8 = bf16[4,64,8,512]{3,2,0,1:T(8,128)(2,1)} copy(bf16[4,64,8,512]{3,2,1,0:T(8,128)(2,1)S(1)} %broadcast_select_fusion) | data formatting | bytes 4194304 | tf_op jit(solution)/shard_map/jit(_take)/select_n | solution.py:41
  42.9 6.9 %all-to-all-start.2 = ((bf16[4,64,8,512]{3,2,0,1:T(8,128)(2,1)}), bf16[4,64,8,512]{3,2,0,1:T(8,128)(2,1)}, u32[]{:S(2)}, u32[]{:S(2)}) async-start(bf16[4,64,8,512]{3,2,0,1:T(8,128)(2,1)} %copy.8), calls=%async_computation.2 | async-start | bytes 4194304 | tf_op jit(solution)/shard_map/all_to_all | solution.py:42
  49.9 1.3 dynamic_slice.13
  51.1 50.0 %all-to-all-done.2 = bf16[4,64,8,512]{3,2,0,1:T(8,128)(2,1)} async-done(((bf16[4,64,8,512]{3,2,0,1:T(8,128)(2,1)}), bf16[4,64,8,512]{3,2,0,1:T(8,128)(2,1)}, u32[]{:S(2)}, u32[]{:S(2)}) %all-to-all-start.2) | async-done | bytes 2097184 | tf_op jit(solution)/shard_map/all_to_all | solution.py:42
  101.1 1.8 %copy.11 = bf16[4,64,8,512]{3,2,1,0:T(8,128)(2,1)S(1)} copy(bf16[4,64,8,512]{3,2,0,1:T(8,128)(2,1)} %all-to-all-done.2) | data formatting | bytes 4194304 | tf_op jit(solution)/shard_map/all_to_all | solution.py:42
  102.9 0.1 broadcast_in_dim.30
  103.0 3.1 %while.10 = (s32[]{:T(128)}, f32[512,512]{1,0:T(8,128)S(1)}, s32[]{:T(128)}, bf16[4,512,512]{2,1,0:T(8,128)(2,1)}, bf16[4,512,512]{2,1,0:T(8,128)(2,1)S(1)}, /*i...) while((s32[]{:T(128)}, f32[512,512]{1,0:T(8,128)S(1)}, s32[]{:T(128)}, ...), condition=%wide.region_1.2_spmd, body=%wide.region_0.1_spmd.sunk | while | flops 537395200 | bytes 3671679 | solution.py:62
  103.6 1.9 %convolution_add_fusion.2 = f32[512,512]{1,0:T(8,128)S(1)} fusion(f32[512,512]{1,0:T(8,128)S(1)} %get-tuple-element.99, bf16[4,512,512]{2,1,0:T(8,128)(2,1)} %get-tuple-element.112, s32[]{:T(128)S(6)} %select_n.30, bf16[4,512,512]{2,1,0:T(8,128)(2,1)S(1)} %get-tuple-element.111, bf16[4,512,512]{2,1,0:T(8,128)(2,1)} %get-tuple-element.110), kind=kOutput, calls=%fused_computation.1.clone.1 | convolution fusion | flops 537395200 | bytes 3671552 | tf_op jit(solution)/shard_map/while/body/dot_general | solution.py:56
  106.1 41.7 %all_to_all.25 = f32[64,8,512]{2,1,0:T(8,128)S(1)} all-to-all(f32[64,8,512]{2,1,0:T(8,128)S(1)} %bitcast.31), channel_id=1, replica_groups=mesh['op'=64,'sec'=8] {'op'}, dimensions={0} | all-to-all | bytes 2097152 | tf_op jit(solution)/shard_map/all_to_all | solution.py:31
  147.9 0.1 reduce_sum.9
  148.0 0.6 fusion.12
  (3 shorter events, 0.0 us)
Async XLA Ops:
  22.7 17.4 %all-to-all-start.1 = ((bf16[8,1,8,512]{3,2,1,0:T(8,128)(2,1)}), bf16[8,1,8,512]{3,2,1,0:T(8,128)(2,1)S(1)}, u32[]{:S(2)}, u32[]{:S(2)}) async-start(bf16[8,1,8,512]{3,2,1,0:T(8,128)(2,1)} %broadcast_in_dim.34), calls=%async_computation.1 | async-start | bytes 131072 | tf_op jit(solution)/shard_map/all_to_all | solution.py:15
  42.9 58.2 %all-to-all-start.2 = ((bf16[4,64,8,512]{3,2,0,1:T(8,128)(2,1)}), bf16[4,64,8,512]{3,2,0,1:T(8,128)(2,1)}, u32[]{:S(2)}, u32[]{:S(2)}) async-start(bf16[4,64,8,512]{3,2,0,1:T(8,128)(2,1)} %copy.8), calls=%async_computation.2 | async-start | bytes 4194304 | tf_op jit(solution)/shard_map/all_to_all | solution.py:42
where the time goes:
time: 149 us
  blocking collectives  62.5 us (42%)
  waiting for transfers between devices  57 us (38%)
  starting transfers between devices  17 us (11%)
  local copies, waits for them, and re-layouts  7.76 us (5%)
  matrix products  1.94 us (1%)
    all_to_all x1, waiting for transfers between devices, shards(): lax.all_to_all(picked, 'op', split_axis=1, concat_axis=1, tiled=True)  50 us
    all_to_all x1, blocking collectives, sum_at_owner(): lax.all_to_all(in_blocks(value, dim, devices), axis, 0, 0, tiled=True)  41.7 us
    all_to_all x1, blocking collectives, copy_for_each(): lax.all_to_all(jnp.broadcast_to(value[None], (devices, *value.shape)), ax...  20.7 us
    all_to_all x1, starting transfers between devices, copy_for_each(): lax.all_to_all(jnp.broadcast_to(value[None], (devices, *value.shape)), ax...  10 us
    all_to_all x1, waiting for transfers between devices, copy_for_each(): lax.all_to_all(jnp.broadcast_to(value[None], (devices, *value.shape)), ax...  7.02 us
    all_to_all x1, starting transfers between devices, shards(): lax.all_to_all(picked, 'op', split_axis=1, concat_axis=1, tiled=True)  6.94 us
  transfers between devices with their start and end apart: 2, of which 2 were waited for; matrix products, arithmetic and copies ran while one was open for 1% of the time, Pallas kernels for 0%

commit v1 on v0

v1 whole, which is shorter than its diff:
```python
import functools

import jax
import jax.numpy as jnp
from jax import lax
from jax.experimental import pallas as pl
from jax.experimental.pallas import tpu as pltpu
from jax.sharding import PartitionSpec as P

MESH = pl.DeviceIdType.MESH
NX, NY, NZ, NC = 4, 8, 8, 2
SIZES = {"x": NX, "y": NY, "z": NZ}
COLS = 128
UNITS = 4
CHUNKS = 2
ORDERS = (("z", "x", "y"), ("x", "y", "z"), ("z", "y", "x"), ("z", "x", "y"))


def kernel(
    wave_ref, left_ref, right_ref, sector_ref, counts_ref, out_ref,
    wbuf, lbuf, rbuf, pbuf, sibling_in, x_out, x_in, y_out, y_in,
    op_sem, own_sem, first_send, first_recv, second_send, second_recv,
    ring_send, ring_recv, twin_send, twin_recv,
    half_send, half_recv, x_send, x_recv, y_send, y_recv,
):
    op = lax.axis_index("op")
    z = lax.axis_index("sec")
    core = lax.rem(op, NC)
    y = lax.rem(lax.div(op, NC), NY)
    x = lax.div(op, NC * NY)
    me = {"x": x, "y": y, "z": z}
    twin = 1 - core
    slots = left_ref.shape[0]

    def device(place, which=None):
        which = core if which is None else which
        return {"op": (place["x"] * NY + place["y"]) * NC + which, "sec": place["z"]}

    def shifted(axis, by):
        n = SIZES[axis]
        return {**me, axis: lax.rem(me[axis] + (by % n), n)}

    def part(unit, place, which=None):
        which = core if which is None else which
        return wbuf.at[unit, place["z"], place["x"], place["y"], which]

    def send(src, dst, send_sem, recv_sem, to):
        pltpu.make_async_remote_copy(
            src_ref=src, dst_ref=dst, send_sem=send_sem, recv_sem=recv_sem,
            device_id=to, device_id_type=MESH,
        ).start()

    def take(ref, sem):
        pltpu.make_async_copy(ref, ref, sem).wait()

    loads = []
    for slot in range(slots):
        loads.append(pltpu.make_async_copy(left_ref.at[slot], lbuf.at[slot], op_sem.at[0, slot]))
        loads.append(pltpu.make_async_copy(right_ref.at[slot], rbuf.at[slot], op_sem.at[1, slot]))
    own = [
        pltpu.make_async_copy(wave_ref.at[0, :, pl.ds(COLS * unit, COLS)], part(unit, me), own_sem.at[unit])
        for unit in range(UNITS)
    ]
    for copy in own:
        copy.start()

    barrier = pltpu.get_barrier_semaphore()
    greeted = 1
    pl.semaphore_signal(barrier, inc=1, device_id=device(me, twin), device_id_type=MESH)
    for axis, n in SIZES.items():
        for by in range(1, n):
            pl.semaphore_signal(barrier, inc=1, device_id=device(shifted(axis, by)), device_id_type=MESH)
            greeted += 1
    for copy in loads:
        copy.start()
    pl.semaphore_wait(barrier, greeted)

    for unit, (first, _, _) in enumerate(ORDERS):
        for by in range(1, SIZES[first]):
            send(
                wave_ref.at[0, :, pl.ds(COLS * unit, COLS)], part(unit, me),
                first_send.at[unit], first_recv.at[unit], device(shifted(first, by)),
            )
    for unit, (first, second, _) in enumerate(ORDERS):
        rest = {**me, first: pl.ds(0, SIZES[first] - 1)}
        take(part(unit, rest), first_recv.at[unit])
        own[unit].wait()
        held = {**me, first: slice(None)}
        for by in range(1, SIZES[second]):
            send(
                part(unit, held), part(unit, held),
                second_send.at[unit], second_recv.at[unit], device(shifted(second, by)),
            )

    def slab(unit, origin, chunk, which=None):
        first, second, third = ORDERS[unit]
        length = SIZES[first] // CHUNKS
        return part(
            unit, {first: pl.ds(chunk * length, length), second: slice(None), third: origin}, which
        )

    def hand_over(unit, origin, chunk):
        piece = slab(unit, origin, chunk)
        send(piece, piece, twin_send.at[unit], twin_recv.at[unit], device(me, twin))

    def pieces(unit, step):
        half = SIZES[ORDERS[unit][2]] // 2
        if step > half:
            return ()
        if step == half:
            return tuple((chunk, 1 if chunk < CHUNKS // 2 else -1) for chunk in range(CHUNKS))
        return tuple((chunk, way) for chunk in range(CHUNKS) for way in (1, -1))

    def pass_on(unit, step, chunk, way):
        third = ORDERS[unit][2]
        origin = shifted(third, -way * (step - 1))[third]
        piece = slab(unit, origin, chunk)
        sem = ring_recv.at[unit, step - 1, chunk, (1 - way) // 2]
        send(piece, piece, ring_send.at[unit], sem, device(shifted(third, way)))

    for unit, (first, second, third) in enumerate(ORDERS):
        rest = {**me, first: slice(None), second: pl.ds(0, SIZES[second] - 1)}
        take(part(unit, rest), second_recv.at[unit])
        for chunk, way in pieces(unit, 1):
            pass_on(unit, 1, chunk, way)
        for chunk in range(CHUNKS):
            hand_over(unit, me[third], chunk)
    for step in range(1, max(SIZES.values()) // 2 + 1):
        for unit, (_, _, third) in enumerate(ORDERS):
            later = pieces(unit, step + 1)
            for chunk, way in pieces(unit, step):
                origin = shifted(third, -way * step)[third]
                take(slab(unit, origin, chunk), ring_recv.at[unit, step - 1, chunk, (1 - way) // 2])
                if (chunk, way) in later:
                    pass_on(unit, step + 1, chunk, way)
                hand_over(unit, origin, chunk)
    everything = {"x": slice(None), "y": slice(None), "z": slice(None)}
    for unit in range(UNITS):
        take(part(unit, everything, twin), twin_recv.at[unit])

    for copy in loads:
        copy.wait()
    alive_below = counts_ref[op, z]
    total = None
    for slot in range(slots):
        sector = sector_ref[slot]
        block = jnp.concatenate(
            [
                wbuf[unit, sector].astype(jnp.float32).reshape(-1, COLS).astype(jnp.bfloat16)
                for unit in range(UNITS)
            ],
            axis=1,
        )
        halfway = jnp.dot(lbuf[slot], block, preferred_element_type=jnp.float32)
        halfway = jnp.where(slot < alive_below, halfway, 0.0).astype(jnp.bfloat16)
        product = lax.dot_general(
            halfway, rbuf[slot], (((1,), (1,)), ((), ())), preferred_element_type=jnp.float32
        )
        total = product if total is None else total + product
    pbuf[...] = total.reshape(pbuf.shape)

    for by in range(NX):
        row = shifted("x", by)["x"]
        send(
            pbuf.at[row, :, twin], sibling_in.at[row], half_send, half_recv.at[by], device(me, twin)
        )
    kept = None
    for by in (*range(1, NX), 0):
        row = shifted("x", by)["x"]
        take(sibling_in.at[row], half_recv.at[by])
        both = pbuf[row, :, core] + sibling_in[row]
        if by:
            x_out[by - 1] = both.astype(jnp.bfloat16)
            send(
                x_out.at[by - 1], x_in.at[by - 1], x_send, x_recv.at[by - 1], device(shifted("x", by))
            )
        else:
            kept = both
    for by in range(1, NX):
        take(x_in.at[by - 1], x_recv.at[by - 1])
        kept = kept + x_in[by - 1].astype(jnp.float32)
    pbuf[x, :, core] = kept
    for by in range(1, NY):
        y_out[by - 1] = pbuf[x, shifted("y", by)["y"], core].astype(jnp.bfloat16)
        send(
            y_out.at[by - 1], y_in.at[by - 1], y_send, y_recv.at[by - 1], device(shifted("y", by))
        )
    result = pbuf[x, y, core]
    for by in range(1, NY):
        take(y_in.at[by - 1], y_recv.at[by - 1])
        result = result + y_in[by - 1].astype(jnp.float32)
    out_ref[0] = (result * (NX * NY * NC * slots) ** -0.5).astype(out_ref.dtype)

    for unit, (first, second, third) in enumerate(ORDERS):
        take(part(unit, {**me, first: pl.ds(0, SIZES[first] - 1)}), first_send.at[unit])
        take(
            part(unit, {**me, first: slice(None), second: pl.ds(0, SIZES[second] - 1)}),
            second_send.at[unit],
        )
        take(part(unit, {**everything, third: pl.ds(0, SIZES[third] - 1)}), ring_send.at[unit])
        take(part(unit, everything), twin_send.at[unit])
    take(sibling_in, half_send)
    take(x_out, x_send)
    take(y_out, y_send)


def shards(wavefunction, left_ops, right_ops, in_sector, counts):
    slots, rows, depth = left_ops.shape
    held = wavefunction.shape[1]
    columns = wavefunction.shape[2]
    dma = pltpu.SemaphoreType.DMA
    steps = max(SIZES.values()) // 2
    return pl.pallas_call(
        kernel,
        out_shape=jax.ShapeDtypeStruct(wavefunction.shape, wavefunction.dtype),
        in_specs=[
            pl.BlockSpec(memory_space=pltpu.VMEM),
            pl.BlockSpec(memory_space=pl.ANY),
            pl.BlockSpec(memory_space=pl.ANY),
            pl.BlockSpec(memory_space=pltpu.SMEM),
            pl.BlockSpec(memory_space=pltpu.SMEM),
        ],
        out_specs=pl.BlockSpec(memory_space=pltpu.VMEM),
        scratch_shapes=[
            pltpu.VMEM((UNITS, NZ, NX, NY, NC, held, COLS), jnp.bfloat16),
            pltpu.VMEM((slots, rows, depth), jnp.bfloat16),
            pltpu.VMEM((slots, columns, columns), jnp.bfloat16),
            pltpu.VMEM((NX, NY, NC, held, columns), jnp.float32),
            pltpu.VMEM((NX, NY, held, columns), jnp.float32),
            pltpu.VMEM((NX - 1, NY, held, columns), jnp.bfloat16),
            pltpu.VMEM((NX - 1, NY, held, columns), jnp.bfloat16),
            pltpu.VMEM((NY - 1, held, columns), jnp.bfloat16),
            pltpu.VMEM((NY - 1, held, columns), jnp.bfloat16),
            dma((2, slots)),
            dma((UNITS,)),
            dma((UNITS,)),
            dma((UNITS,)),
            dma((UNITS,)),
            dma((UNITS,)),
            dma((UNITS,)),
            dma((UNITS, steps, CHUNKS, 2)),
            dma((UNITS,)),
            dma((UNITS,)),
            dma,
            dma((NX,)),
            dma,
            dma((NX - 1,)),
            dma,
            dma((NY - 1,)),
        ],
        compiler_params=pltpu.CompilerParams(collective_id=0, has_side_effects=True),
    )(wavefunction, left_ops, right_ops, in_sector, counts)


def solution(mesh):
    placed = (
        P("sec", "op", None),
        P(("op", "sec"), None, None),
        P(("op", "sec"), None, None),
        P(("op", "sec")),
        P(),
    )
    return jax.shard_map(
        shards, mesh=mesh, in_specs=placed, out_specs=P("sec", "op", None), check_vma=False
    )
```

time: 149 us -> 60.9 us (0.41)
  the two profiles are of different devices: /device:TPU:1 before, /device:TPU:8 now
where the time goes in v1:
time: 60.9 us; the launch traced here: 60.6 us
  Pallas kernels  57.9 us (95%)
  local copies, waits for them, and re-layouts  2.67 us (4%)
    pallas_call x1, Pallas kernels, shards(): pl.pallas_call(kernel, out_shape=jax.ShapeDtypeStruct(wavefunction.shape,...  57.9 us
    unnamed x2, local copies, waits for them, and re-layouts  2.67 us

profile of v1, /device:TPU:8, one launch (start us, length us, event | category | flops | bytes accessed | tf_op | source)
XLA Modules:
  0.0 60.6 jit_solution(5346708500008267639)
XLA Ops:
  0.0 1.4 %copy.6.counts_ref = s32[64,8]{1,0:T(8,128)} copy(s32[64,8]{0,1:T(8,128)} %param.9) | data formatting | bytes 4096 | tf_op args[4]
  1.4 57.9 %shard_map.55 = bf16[1,8,512]{2,1,0:T(8,128)(2,1)} custom-call(bf16[1,8,512]{2,1,0:T(8,128)(2,1)} %wave_ref.1, bf16[4,512,512]{2,1,0:T(8,128)(2,1)} %left_ref.1, bf16[4,512,512]{2,1,0:T(8,128)(2,1)} %right_ref.1, s32[4]{0:T(128)} %sector_ref.1, s32[64,8]{1,0:T(8,128)} %copy.6.counts_ref), custom_call_target="tpu_custom_call" | custom-call | tf_op jit(solution)/shard_map/pallas_call | solution.py:213
  59.3 1.3 %copy.8 = bf16[1,8,512]{2,1,0:T(8,128)(2,1)} copy(bf16[1,8,512]{2,1,0:T(8,128)(2,1)} %shard_map.55) | data formatting | bytes 16384

commit v2 on v1

v2 whole, which is shorter than its diff:
```python
import functools

import jax
import jax.numpy as jnp
from jax import lax
from jax.experimental import pallas as pl
from jax.experimental.pallas import tpu as pltpu
from jax.sharding import PartitionSpec as P

MESH = pl.DeviceIdType.MESH
NX, NY, NZ, NC = 4, 8, 8, 2
SIZES = {"x": NX, "y": NY, "z": NZ}
COLS = 256
LAST = ("y", "z")
UNITS = len(LAST)
SPREAD = {"y": "z", "z": "y"}
PEERS = NX * NY - 1
OFFSETS = [
    {"x": dx, "y": dy, "z": dz}
    for dx in range(NX)
    for dy in range(NY)
    for dz in range(NZ)
    if (dx or dy or dz) and not (dy and dz)
]


def kernel(
    wave_ref, left_ref, right_ref, sector_ref, counts_ref, out_ref,
    wbuf, lbuf, rbuf, pbuf, sibling_in, share_out, share_in,
    op_sem, own_sem, plane_send, plane_recv,
    ring_send, ring_recv, twin_send, twin_recv,
    half_send, half_recv, share_send, share_recv,
):
    op = lax.axis_index("op")
    z = lax.axis_index("sec")
    core = lax.rem(op, NC)
    y = lax.rem(lax.div(op, NC), NY)
    x = lax.div(op, NC * NY)
    me = {"x": x, "y": y, "z": z}
    twin = 1 - core
    slots = left_ref.shape[0]

    def device(place, which=None):
        which = core if which is None else which
        return {"op": (place["x"] * NY + place["y"]) * NC + which, "sec": place["z"]}

    def shifted(axis, by):
        n = SIZES[axis]
        return {**me, axis: lax.rem(me[axis] + (by % n), n)}

    def moved(offset):
        return {axis: lax.rem(me[axis] + offset[axis], SIZES[axis]) for axis in SIZES}

    def part(unit, place, which=None):
        which = core if which is None else which
        return wbuf.at[unit, place["z"], place["x"], place["y"], which]

    def send(src, dst, send_sem, recv_sem, to):
        pltpu.make_async_remote_copy(
            src_ref=src, dst_ref=dst, send_sem=send_sem, recv_sem=recv_sem,
            device_id=to, device_id_type=MESH,
        ).start()

    def take(ref, sem):
        pltpu.make_async_copy(ref, ref, sem).wait()

    loads = []
    for slot in range(slots):
        loads.append(pltpu.make_async_copy(left_ref.at[slot], lbuf.at[slot], op_sem.at[0, slot]))
        loads.append(pltpu.make_async_copy(right_ref.at[slot], rbuf.at[slot], op_sem.at[1, slot]))
    own = [
        pltpu.make_async_copy(wave_ref.at[0, :, pl.ds(COLS * unit, COLS)], part(unit, me), own_sem.at[unit])
        for unit in range(UNITS)
    ]
    for copy in own:
        copy.start()

    barrier = pltpu.get_barrier_semaphore()
    greeted = 1
    pl.semaphore_signal(barrier, inc=1, device_id=device(me, twin), device_id_type=MESH)
    for offset in OFFSETS:
        pl.semaphore_signal(barrier, inc=1, device_id=device(moved(offset)), device_id_type=MESH)
        greeted += 1
    for copy in loads:
        copy.start()
    for copy in own:
        copy.wait()
    pl.semaphore_wait(barrier, greeted)

    for unit, last in enumerate(LAST):
        for offset in OFFSETS:
            if not offset[last]:
                send(
                    part(unit, me), part(unit, me),
                    plane_send.at[unit], plane_recv.at[unit], device(moved(offset)),
                )

    def slab(unit, chunk, origin):
        last = LAST[unit]
        return part(unit, {"x": chunk, SPREAD[last]: slice(None), last: origin})

    def hand_over(unit, piece):
        send(piece, piece, twin_send.at[unit], twin_recv.at[unit], device(me, twin))

    def ways(chunk, step):
        if step < NY // 2:
            return (1, -1)
        return ((1, -1)[chunk % 2],) if step == NY // 2 else ()

    def ring_sem(unit, chunk, step, way):
        return ring_recv.at[unit, (step - 1) * NX + chunk, (1 - way) // 2]

    def pass_on(unit, chunk, step, way):
        last = LAST[unit]
        piece = slab(unit, chunk, shifted(last, -way * (step - 1))[last])
        send(
            piece, piece, ring_send.at[unit], ring_sem(unit, chunk, step, way),
            device(shifted(last, way)),
        )

    for unit, last in enumerate(LAST):
        take(share_in.at[:, :, pl.ds(0, COLS)], plane_recv.at[unit])
        for chunk in range(NX):
            for way in ways(chunk, 1):
                pass_on(unit, chunk, 1, way)
        for chunk in range(NX):
            hand_over(unit, slab(unit, chunk, me[last]))
    for step in range(1, NY // 2 + 1):
        for unit, last in enumerate(LAST):
            for chunk in range(NX):
                for way in ways(chunk, step):
                    piece = slab(unit, chunk, shifted(last, -way * step)[last])
                    take(piece, ring_sem(unit, chunk, step, way))
                    if way in ways(chunk, step + 1):
                        pass_on(unit, chunk, step + 1, way)
                    hand_over(unit, piece)
    everything = {"x": slice(None), "y": slice(None), "z": slice(None)}
    for unit in range(UNITS):
        take(part(unit, everything, twin), twin_recv.at[unit])

    for copy in loads:
        copy.wait()
    alive_below = counts_ref[z, op]
    total = None
    for slot in range(slots):
        sector = sector_ref[slot]
        block = jnp.concatenate(
            [
                wbuf[unit, sector].astype(jnp.float32).reshape(-1, COLS).astype(jnp.bfloat16)
                for unit in range(UNITS)
            ],
            axis=1,
        )
        halfway = jnp.dot(lbuf[slot], block, preferred_element_type=jnp.float32)
        halfway = jnp.where(slot < alive_below, halfway, 0.0).astype(jnp.bfloat16)
        product = lax.dot_general(
            halfway, rbuf[slot], (((1,), (1,)), ((), ())), preferred_element_type=jnp.float32
        )
        total = product if total is None else total + product
    pbuf[...] = total.reshape(pbuf.shape)

    for by in range(NX):
        row = shifted("x", by)["x"]
        send(
            pbuf.at[row, :, twin], sibling_in.at[row], half_send, half_recv.at[by], device(me, twin)
        )
    for by in (*range(1, NX), 0):
        row = shifted("x", by)["x"]
        take(sibling_in.at[row], half_recv.at[by])
        pbuf[row, :, core] = pbuf[row, :, core] + sibling_in[row]
        share_out[row] = pbuf[row, :, core].astype(jnp.bfloat16)
        for dy in range(NY):
            if by or dy:
                to = moved({"x": by, "y": dy, "z": 0})
                send(
                    share_out.at[to["x"], to["y"]], share_in.at[by * NY + dy - 1],
                    share_send, share_recv, device(to),
                )
    take(share_in, share_recv)
    result = pbuf[x, y, core] + jnp.sum(share_in[...].astype(jnp.float32), axis=0)
    out_ref[0] = (result * (NX * NY * NC * slots) ** -0.5).astype(out_ref.dtype)

    for unit, last in enumerate(LAST):
        take(share_in.at[:, :, pl.ds(0, COLS)], plane_send.at[unit])
        take(part(unit, {**everything, last: pl.ds(0, SIZES[last] - 1)}), ring_send.at[unit])
        take(part(unit, everything), twin_send.at[unit])
    take(sibling_in, half_send)
    take(share_in, share_send)


def shards(wavefunction, left_ops, right_ops, in_sector, counts):
    slots, rows, depth = left_ops.shape
    held = wavefunction.shape[1]
    columns = wavefunction.shape[2]
    dma = pltpu.SemaphoreType.DMA
    return pl.pallas_call(
        kernel,
        out_shape=jax.ShapeDtypeStruct(wavefunction.shape, wavefunction.dtype),
        in_specs=[
            pl.BlockSpec(memory_space=pltpu.VMEM),
            pl.BlockSpec(memory_space=pl.ANY),
            pl.BlockSpec(memory_space=pl.ANY),
            pl.BlockSpec(memory_space=pltpu.SMEM),
            pl.BlockSpec(memory_space=pltpu.SMEM),
        ],
        out_specs=pl.BlockSpec(memory_space=pltpu.VMEM),
        scratch_shapes=[
            pltpu.VMEM((UNITS, NZ, NX, NY, NC, held, COLS), jnp.bfloat16),
            pltpu.VMEM((slots, rows, depth), jnp.bfloat16),
            pltpu.VMEM((slots, columns, columns), jnp.bfloat16),
            pltpu.VMEM((NX, NY, NC, held, columns), jnp.float32),
            pltpu.VMEM((NX, NY, held, columns), jnp.float32),
            pltpu.VMEM((NX, NY, held, columns), jnp.bfloat16),
            pltpu.VMEM((PEERS, held, columns), jnp.bfloat16),
            dma((2, slots)),
            dma((UNITS,)),
            dma((UNITS,)),
            dma((UNITS,)),
            dma((UNITS,)),
            dma((UNITS, NX * NY // 2, 2)),
            dma((UNITS,)),
            dma((UNITS,)),
            dma,
            dma((NX,)),
            dma,
            dma,
        ],
        compiler_params=pltpu.CompilerParams(collective_id=0, has_side_effects=True),
    )(wavefunction, left_ops, right_ops, in_sector, counts.T)


def solution(mesh):
    placed = (
        P("sec", "op", None),
        P(("op", "sec"), None, None),
        P(("op", "sec"), None, None),
        P(("op", "sec")),
        P(),
    )
    return jax.shard_map(
        shards, mesh=mesh, in_specs=placed, out_specs=P("sec", "op", None), check_vma=False
    )
```

time: 60.9 us -> 56.2 us (0.923)
  the two profiles are of different devices: /device:TPU:8 before, /device:TPU:16 now
where the time goes in v2:
time: 56.2 us; the launch traced here: 56 us
  Pallas kernels  54.7 us (97%)
  local copies, waits for them, and re-layouts  1.3 us (2%)
    pallas_call x1, Pallas kernels, shards(): pl.pallas_call(kernel, out_shape=jax.ShapeDtypeStruct(wavefunction.shape,...  54.7 us
    unnamed x1, local copies, waits for them, and re-layouts  1.3 us

profile of v2, /device:TPU:16, one launch (start us, length us, event | category | flops | bytes accessed | tf_op | source)
XLA Modules:
  0.0 56.0 jit_solution(12422557593861835828)
XLA Ops:
  0.0 54.7 %shard_map.55 = bf16[1,8,512]{2,1,0:T(8,128)(2,1)} custom-call(bf16[1,8,512]{2,1,0:T(8,128)(2,1)} %wave_ref.1, bf16[4,512,512]{2,1,0:T(8,128)(2,1)} %left_ref.1, bf16[4,512,512]{2,1,0:T(8,128)(2,1)} %right_ref.1, s32[4]{0:T(128)} %sector_ref.1, s32[8,64]{1,0:T(8,128)} %bitcast.1), custom_call_target="tpu_custom_call" | custom-call | tf_op jit(solution)/shard_map/pallas_call | solution.py:196
  54.7 1.3 %copy.7 = bf16[1,8,512]{2,1,0:T(8,128)(2,1)} copy(bf16[1,8,512]{2,1,0:T(8,128)(2,1)} %shard_map.55) | data formatting | bytes 16384

commit v3 on v2

--- a/solution.py
+++ b/solution.py
@@ -15,20 +15,29 @@
 UNITS = len(LAST)
 SPREAD = {"y": "z", "z": "y"}
 PEERS = NX * NY - 1
-OFFSETS = [
-    {"x": dx, "y": dy, "z": dz}
-    for dx in range(NX)
-    for dy in range(NY)
-    for dz in range(NZ)
-    if (dx or dy or dz) and not (dy and dz)
-]
+
+
+def hops(offset):
+    return sum(min(by, SIZES[axis] - by) for axis, by in offset.items())
+
+
+OFFSETS = sorted(
+    (
+        {"x": dx, "y": dy, "z": dz}
+        for dx in range(NX)
+        for dy in range(NY)
+        for dz in range(NZ)
+        if (dx or dy or dz) and not (dy and dz)
+    ),
+    key=lambda offset: -hops(offset),
+)
 
 
 def kernel(
     wave_ref, left_ref, right_ref, sector_ref, counts_ref, out_ref,
-    wbuf, lbuf, rbuf, pbuf, sibling_in, share_out, share_in,
+    wbuf, lbuf, rbuf, hbuf, pbuf, sibling_in, share_out, share_in,
     op_sem, own_sem, plane_send, plane_recv,
-    ring_send, ring_recv, twin_send, twin_recv,
+    ring_send, ring_recv, edge_recv, twin_send, twin_recv,
     half_send, half_recv, share_send, share_recv,
 ):
     op = lax.axis_index("op")
@@ -117,6 +126,10 @@
             piece, piece, ring_send.at[unit], ring_sem(unit, chunk, step, way),
             device(shifted(last, way)),
         )
+        if step == NY // 2:
+            send(
+                piece, piece, ring_send.at[unit], edge_recv.at[unit], device(shifted(last, way), twin)
+            )
 
     for unit, last in enumerate(LAST):
         take(share_in.at[:, :, pl.ds(0, COLS)], plane_recv.at[unit])
@@ -126,22 +139,24 @@
         for chunk in range(NX):
             hand_over(unit, slab(unit, chunk, me[last]))
     for step in range(1, NY // 2 + 1):
-        for unit, last in enumerate(LAST):
-            for chunk in range(NX):
+        for chunk in range(NX):
+            for unit, last in enumerate(LAST):
                 for way in ways(chunk, step):
                     piece = slab(unit, chunk, shifted(last, -way * step)[last])
                     take(piece, ring_sem(unit, chunk, step, way))
                     if way in ways(chunk, step + 1):
                         pass_on(unit, chunk, step + 1, way)
-                    hand_over(unit, piece)
+                    if step < NY // 2:
+                        hand_over(unit, piece)
     everything = {"x": slice(None), "y": slice(None), "z": slice(None)}
     for unit in range(UNITS):
-        take(part(unit, everything, twin), twin_recv.at[unit])
+        most = {**everything, LAST[unit]: pl.ds(0, SIZES[LAST[unit]] - 1)}
+        take(part(unit, most, twin), twin_recv.at[unit])
+        take(part(unit, {**everything, LAST[unit]: 0}, twin), edge_recv.at[unit])
 
     for copy in loads:
         copy.wait()
     alive_below = counts_ref[z, op]
-    total = None
     for slot in range(slots):
         sector = sector_ref[slot]
         block = jnp.concatenate(
@@ -152,24 +167,33 @@
             axis=1,
         )
         halfway = jnp.dot(lbuf[slot], block, preferred_element_type=jnp.float32)
-        halfway = jnp.where(slot < alive_below, halfway, 0.0).astype(jnp.bfloat16)
-        product = lax.dot_general(
-            halfway, rbuf[slot], (((1,), (1,)), ((), ())), preferred_element_type=jnp.float32
-        )
-        total = product if total is None else total + product
-    pbuf[...] = total.reshape(pbuf.shape)
-
-    for by in range(NX):
-        row = shifted("x", by)["x"]
-        send(
-            pbuf.at[row, :, twin], sibling_in.at[row], half_send, half_recv.at[by], device(me, twin)
-        )
-    for by in (*range(1, NX), 0):
+        hbuf[slot] = jnp.where(slot < alive_below, halfway, 0.0).astype(jnp.bfloat16)
+
+    length = hbuf.shape[1] // NX
+    for pair in ((2, 1), (3, 0)):
+        rows = [shifted("x", by)["x"] for by in pair]
+        total = None
+        for slot in range(slots):
+            halfway = jnp.concatenate(
+                [hbuf[slot, pl.ds(pl.multiple_of(row * length, length), length)] for row in rows]
+            )
+            product = lax.dot_general(
+                halfway, rbuf[slot], (((1,), (1,)), ((), ())), preferred_element_type=jnp.float32
+            )
+            total = product if total is None else total + product
+        total = total.reshape(len(pair), *pbuf.shape[1:])
+        for place, (by, row) in enumerate(zip(pair, rows)):
+            pbuf[row] = total[place]
+            send(
+                pbuf.at[row, :, twin], sibling_in.at[row], half_send, half_recv.at[by],
+                device(me, twin),
+            )
+    for by in (2, 1, 3, 0):
         row = shifted("x", by)["x"]
         take(sibling_in.at[row], half_recv.at[by])
         pbuf[row, :, core] = pbuf[row, :, core] + sibling_in[row]
         share_out[row] = pbuf[row, :, core].astype(jnp.bfloat16)
-        for dy in range(NY):
+        for dy in (4, 3, 5, 2, 6, 1, 7, 0):
             if by or dy:
                 to = moved({"x": by, "y": dy, "z": 0})
                 send(
@@ -182,8 +206,8 @@
 
     for unit, last in enumerate(LAST):
         take(share_in.at[:, :, pl.ds(0, COLS)], plane_send.at[unit])
-        take(part(unit, {**everything, last: pl.ds(0, SIZES[last] - 1)}), ring_send.at[unit])
-        take(part(unit, everything), twin_send.at[unit])
+        take(part(unit, everything), ring_send.at[unit])
+        take(part(unit, {**everything, last: pl.ds(0, SIZES[last] - 1)}), twin_send.at[unit])
     take(sibling_in, half_send)
     take(share_in, share_send)
 
@@ -208,6 +232,7 @@
             pltpu.VMEM((UNITS, NZ, NX, NY, NC, held, COLS), jnp.bfloat16),
             pltpu.VMEM((slots, rows, depth), jnp.bfloat16),
             pltpu.VMEM((slots, columns, columns), jnp.bfloat16),
+            pltpu.VMEM((slots, rows, columns), jnp.bfloat16),
             pltpu.VMEM((NX, NY, NC, held, columns), jnp.float32),
             pltpu.VMEM((NX, NY, held, columns), jnp.float32),
             pltpu.VMEM((NX, NY, held, columns), jnp.bfloat16),
@@ -218,6 +243,7 @@
             dma((UNITS,)),
             dma((UNITS,)),
             dma((UNITS, NX * NY // 2, 2)),
+            dma((UNITS,)),
             dma((UNITS,)),
             dma((UNITS,)),
             dma,

time: 56.2 us -> 53.7 us (0.956)
  the two profiles are of different devices: /device:TPU:16 before, /device:TPU:1 now
where the time goes in v3:
time: 53.7 us; the launch traced here: 53.4 us
  Pallas kernels  52.1 us (97%)
  local copies, waits for them, and re-layouts  1.3 us (2%)
    pallas_call x1, Pallas kernels, shards(): pl.pallas_call(kernel, out_shape=jax.ShapeDtypeStruct(wavefunction.shape,...  52.1 us
    unnamed x1, local copies, waits for them, and re-layouts  1.3 us

profile of v3, /device:TPU:1, one launch (start us, length us, event | category | flops | bytes accessed | tf_op | source)
XLA Modules:
  0.0 53.4 jit_solution(18293766317090555521)
XLA Ops:
  0.0 52.1 %shard_map.55 = bf16[1,8,512]{2,1,0:T(8,128)(2,1)} custom-call(bf16[1,8,512]{2,1,0:T(8,128)(2,1)} %wave_ref.1, bf16[4,512,512]{2,1,0:T(8,128)(2,1)} %left_ref.1, bf16[4,512,512]{2,1,0:T(8,128)(2,1)} %right_ref.1, s32[4]{0:T(128)} %sector_ref.1, s32[8,64]{1,0:T(8,128)} %bitcast.1), custom_call_target="tpu_custom_call" | custom-call | tf_op jit(solution)/shard_map/pallas_call | solution.py:220
  52.1 1.3 %copy.7 = bf16[1,8,512]{2,1,0:T(8,128)(2,1)} copy(bf16[1,8,512]{2,1,0:T(8,128)(2,1)} %shard_map.55) | data formatting | bytes 16384

commit v4 on v3

--- a/solution.py
+++ b/solution.py
@@ -90,19 +90,20 @@
     for offset in OFFSETS:
         pl.semaphore_signal(barrier, inc=1, device_id=device(moved(offset)), device_id_type=MESH)
         greeted += 1
-    for copy in loads:
-        copy.start()
     for copy in own:
         copy.wait()
     pl.semaphore_wait(barrier, greeted)
 
-    for unit, last in enumerate(LAST):
-        for offset in OFFSETS:
+    for offset in OFFSETS:
+        for unit, last in enumerate(LAST):
             if not offset[last]:
                 send(
                     part(unit, me), part(unit, me),
                     plane_send.at[unit], plane_recv.at[unit], device(moved(offset)),
                 )
+
+    for copy in loads:
+        copy.start()
 
     def slab(unit, chunk, origin):
         last = LAST[unit]
@@ -161,7 +162,7 @@
         sector = sector_ref[slot]
         block = jnp.concatenate(
             [
-                wbuf[unit, sector].astype(jnp.float32).reshape(-1, COLS).astype(jnp.bfloat16)
+                wbuf[unit, sector].reshape(-1, COLS)
                 for unit in range(UNITS)
             ],
             axis=1,

time: 53.7 us -> 53.6 us (level)
  no operation moved by 1% of the time
where the time goes in v4:
time: 53.6 us; the launch traced here: 53.4 us
  Pallas kernels  52.1 us (97%)
  local copies, waits for them, and re-layouts  1.3 us (2%)
    pallas_call x1, Pallas kernels, shards(): pl.pallas_call(kernel, out_shape=jax.ShapeDtypeStruct(wavefunction.shape,...  52.1 us
    unnamed x1, local copies, waits for them, and re-layouts  1.3 us

profile of v4, /device:TPU:1, one launch (start us, length us, event | category | flops | bytes accessed | tf_op | source)
XLA Modules:
  0.0 53.4 jit_solution(11111075061618965562)
XLA Ops:
  0.0 52.1 %shard_map.55 = bf16[1,8,512]{2,1,0:T(8,128)(2,1)} custom-call(bf16[1,8,512]{2,1,0:T(8,128)(2,1)} %wave_ref.1, bf16[4,512,512]{2,1,0:T(8,128)(2,1)} %left_ref.1, bf16[4,512,512]{2,1,0:T(8,128)(2,1)} %right_ref.1, s32[4]{0:T(128)} %sector_ref.1, s32[8,64]{1,0:T(8,128)} %bitcast.1), custom_call_target="tpu_custom_call" | custom-call | tf_op jit(solution)/shard_map/pallas_call | solution.py:221
  52.1 1.3 %copy.7 = bf16[1,8,512]{2,1,0:T(8,128)(2,1)} copy(bf16[1,8,512]{2,1,0:T(8,128)(2,1)} %shard_map.55) | data formatting | bytes 16384
